TPU v7x, 32 devices: a whole 2x2x4 slice. The times are simulated.
32 devices in a mesh: video: 2 (over x), tm: 16 (over z, y, core).
Axes of the slice: x: 2, y: 2, z: 4, core: 2. Of those that a mesh axis runs over, the one named last changes fastest.
Arguments:
- video: bfloat16 [32, 3, 32, 960], P(('video', 'tm')), parts along dimension 0, may hold values from -6 to 6
- w_in: float32 [32, 3], replicated, may hold values from -3.5 to 3.5
- b_in: float32 [32], replicated, may hold values from -2 to 2
- w_out: float32 [3, 32], replicated, may hold values from -1 to 1
- b_out: float32 [3], replicated, may hold values from -2 to 2
- screen: float32 [3], replicated, may hold values from 0.5 to 2
Outputs:
- consistent: float32 [32, 3, 32, 960], P('video', None, 'tm'), parts along dimension 0
There are 2 independent parts, one for each index of `video`. A program takes and returns all parts, laid end to end along the dimension named above; an argument that names none is the same for every part. Nothing has to cross between parts.
All inputs are finite; a program needn't handle non-finite values.
Results may differ from a plain program's by a relative error of at most 0.0036.
Values may be sent and summed in bfloat16 or wider, within the bound.
A program may use at most 64 MiB of HBM per device.

v0:
```python
import functools

import jax
import jax.numpy as jnp
from jax import lax
from jax.experimental import pallas as pl
from jax.experimental.pallas import tpu as pltpu
from jax.sharding import PartitionSpec as P

ITERS = 3
LANES = 128
HELD = 1
HALO = ITERS + 1


def blocks_of(count, size):
    return [(start, min(size, count - start)) for start in range(0, count, size)]


def partner(index, step, count):
    if count & (count - 1):
        return lax.rem(index + count // 2 + step, count)
    mask, found, bit = count - 1 - step, 0, 1
    while bit < count:
        found = found + lax.rem(index // bit + mask // bit, 2) * bit
        bit *= 2
    return found


def shifted(field, axis, step):
    size = field.shape[axis]
    index = lax.broadcasted_iota(jnp.int32, field.shape, axis)
    moved = pltpu.roll(field, 1 if step == 1 else size - 1, axis)
    return jnp.where(index == (0 if step == 1 else size - 1), 0.0, moved)


def coefficients(m):
    a0 = m[0] / m[1]
    rr1 = m[0] - 2.0 * a0 * m[1] + a0 * a0 * m[2]
    p10, p11 = 1.0 + rr1 / m[0], -a0
    a1 = rr1 / (p10 * p10 * m[1] + 2.0 * p10 * p11 * m[2] + p11 * p11 * m[3])
    r1, r2 = -a0 - a1 * p10, -a1 * p11
    rr2 = m[0] + r1 * r1 * m[2] + r2 * r2 * m[4] + 2.0 * (r1 * m[1] + r2 * m[2] + r1 * r2 * m[3])
    beta = rr2 / rr1
    p20, p21, p22 = 1.0 + beta * p10, r1 + beta * p11, r2
    bottom = (
        p20 * p20 * m[1]
        + p21 * p21 * m[3]
        + p22 * p22 * m[5]
        + 2.0 * (p20 * p21 * m[2] + p20 * p22 * m[3] + p21 * p22 * m[4])
    )
    a2 = rr2 / bottom
    return a0 + a1 * p10 + a2 * p20, a1 * p11 + a2 * p21, a2 * p22


def kernel(
    count,
    video_hbm, w_in_hbm, b_in_hbm, w_out_hbm, b_out_hbm, screen_hbm,
    recv2,
    video_ref, w_in_ref, b_in_ref, w_out_ref, b_out_ref, screen_ref, load_sem,
    wide, pieces, packed, send1, recv1, flat, power0, power1, power2,
    mine, sums, send2,
    send1_sem, recv1_sem, sum_send_sem, sum_recv_sem, send2_sem, recv2_sem, local_sem,
):
    me = lax.axis_index("tm")
    chips = count // 2
    chip, core = me // 2, lax.rem(me, 2)
    _, channels, rows, cols = video_ref.shape
    units = w_in_ref.shape[1]
    frames = count
    own = cols // chips
    half = rows // 2
    window = half + ITERS
    chunk = send1.shape[1]
    band = rows // count
    bands = count // 2

    barrier = pltpu.get_barrier_semaphore()

    def greet(step, carry):
        pl.semaphore_signal(barrier, inc=1, device_id={"tm": lax.rem(me + step, count)})
        return carry

    loads = [
        pltpu.make_async_copy(source, dest, load_sem.at[i])
        for i, (source, dest) in enumerate(
            (
                (video_hbm, video_ref),
                (w_in_hbm, w_in_ref),
                (b_in_hbm, b_in_ref),
                (w_out_hbm, w_out_ref),
                (b_out_hbm, b_out_ref),
                (screen_hbm, screen_ref),
            )
        )
    ]
    for load in loads:
        load.start()
    lax.fori_loop(1, count, greet, 0)
    for load in loads:
        load.wait()

    tiles = wide.shape[2] // LANES
    for c in range(channels):
        wide[c, :, :LANES] = jnp.zeros((rows, LANES), jnp.float32)
        for t in range(1 + cols // LANES, tiles):
            wide[c, :, t * LANES:(t + 1) * LANES] = jnp.zeros((rows, LANES), jnp.float32)
        wide[c, :, LANES:LANES + cols] = video_ref[0, c].astype(jnp.float32)
    lane2 = lax.broadcasted_iota(jnp.int32, (rows, LANES), 1)
    for k in range(chips):
        tile, offset = divmod(LANES + own * k - HALO, LANES)
        for c in range(channels):
            first = wide[c, :, tile * LANES:(tile + 1) * LANES]
            if offset:
                second = wide[c, :, (tile + 1) * LANES:(tile + 2) * LANES]
                first = pltpu.roll(first, LANES - offset, 1)
                second = pltpu.roll(second, LANES - offset, 1)
                first = jnp.where(lane2 < LANES - offset, first, second)
            pieces[k, c] = first
    packed[...] = jnp.zeros_like(packed)

    def grade(k):
        column = lane2 + (own * k - HALO)
        inside = jnp.logical_and(column >= 0, column < cols)
        parts = [[] for _ in range(channels)]
        for start, size in blocks_of(rows, 32):
            pixels = [pieces[k, c, start:start + size, :] for c in range(channels)]
            total = [pixels[c] + b_out_ref[c] for c in range(channels)]
            for j in range(units):
                h = pixels[0] * (0.5 * w_in_ref[0, j]) + 0.5 * b_in_ref[j]
                for c in range(1, channels):
                    h = h + pixels[c] * (0.5 * w_in_ref[c, j])
                act = h * jnp.tanh(h) + h
                for c in range(channels):
                    total[c] = total[c] + act * w_out_ref[c, j]
            for c in range(channels):
                parts[c].append(total[c])
        for c in range(channels):
            graded = parts[c][0] if len(parts[c]) == 1 else jnp.concatenate(parts[c], 0)
            graded = jnp.where(inside, graded, 0.0)
            beside = shifted(graded, 0, 1) + shifted(graded, 0, -1)
            beside = beside + pltpu.roll(graded, 1, 1) + pltpu.roll(graded, LANES - 1, 1)
            target = jnp.where(inside, (screen_ref[c] + 4.0) * graded - beside, 0.0)
            packed[0, c * window:(c + 1) * window, :] = target[:window]
            packed[1, c * window:(c + 1) * window, :] = target[rows - window:]

    def copy1(dest):
        return pltpu.make_async_remote_copy(
            src_ref=send1.at[dest],
            dst_ref=recv1.at[me],
            send_sem=send1_sem.at[dest],
            recv_sem=recv1_sem.at[me],
            device_id={"tm": dest},
        )

    def arrival1(source):
        return pltpu.make_async_remote_copy(
            src_ref=send1.at[source],
            dst_ref=recv1.at[source],
            send_sem=send1_sem.at[source],
            recv_sem=recv1_sem.at[source],
            device_id={"tm": source},
        )

    held = min(HELD, chips - 1)

    def launch(k):
        for side in range(2):
            dest = 2 * k + side

            @pl.when(dest != me)
            def _():
                copy1(dest).start()

    def make(step, carry):
        k = lax.rem(chip + chips // 2 + step, chips)
        grade(k)
        for side in range(2):
            send1[2 * k + side] = packed[side].astype(jnp.bfloat16)

        @pl.when(step == held)
        def _():
            pl.semaphore_wait(barrier, count - 1)
            for earlier in range(held):
                launch(lax.rem(chip + chips // 2 + earlier, chips))

        @pl.when(step >= held)
        def _():
            launch(k)

        return carry

    lax.fori_loop(0, chips, make, 0)
    recv1[me] = send1[me]

    def land(step, carry):
        source = lax.rem(me + step, count)

        @pl.when(step > 0)
        def _():
            arrival1(source).wait_recv()

        flat[pl.ds(pl.multiple_of(source * chunk, chunk), chunk), :] = recv1[source].astype(jnp.float32)
        return carry

    lax.fori_loop(0, count, land, 0)

    lane = lax.broadcasted_iota(jnp.int32, (1, frames, LANES), 2)
    column = lane + (own * chip - HALO)
    inside = jnp.logical_and(column >= 0, column < cols)
    owned = jnp.logical_and(lane >= HALO, lane < HALO + own)
    frame = lax.broadcasted_iota(jnp.int32, (1, frames, LANES), 1)

    for power in (power0, power1, power2):
        for c in range(channels):
            power[c, 0] = jnp.zeros((frames, LANES), jnp.float32)
            power[c, window + 1] = jnp.zeros((frames, LANES), jnp.float32)
    for c in range(channels):
        for r in range(window):
            power0[c, r + 1] = flat[pl.ds(c * window + r, frames, chunk), :]

    def operate(ref, c, start, size):
        whole = ref[c, pl.ds(start, size + 2)]
        centre = whole[1:size + 1]
        total = whole[:size] + whole[2:]
        total = total + pltpu.roll(centre, 1, 2) + pltpu.roll(centre, LANES - 1, 2)
        before = jnp.where(frame == 0, 0.0, pltpu.roll(centre, 1, 1))
        after = jnp.where(frame == frames - 1, 0.0, pltpu.roll(centre, frames - 1, 1))
        total = total + before + after
        return centre, (6.0 + screen_ref[c]) * centre - total

    shift = core * ITERS
    for ref, result in ((power0, power1), (power1, power2)):
        def apply(c, carry, ref=ref, result=result):
            for start, size in blocks_of(window, 4):
                _, image = operate(ref, c, start, size)
                result[c, start + 1:start + 1 + size] = jnp.where(inside, image, 0.0)
            return carry

        lax.fori_loop(0, channels, apply, 0)

    lane1 = lax.broadcasted_iota(jnp.int32, (1, LANES), 1)

    def moments(c, row):
        acc = [jnp.zeros((frames, LANES), jnp.float32) for _ in range(6)]
        for start, size in blocks_of(half, 4):
            v0 = power0[c, pl.ds(shift + start + 1, size)]
            v1 = power1[c, pl.ds(shift + start + 1, size)]
            v2, v3 = operate(power2, c, shift + start, size)
            for i, (left, right) in enumerate(
                ((v0, v0), (v0, v1), (v1, v1), (v1, v2), (v2, v2), (v2, v3))
            ):
                acc[i] = acc[i] + jnp.sum(left * right, axis=0)
        for i in range(6):
            value = jnp.sum(jnp.where(owned[0], acc[i], 0.0), axis=0, keepdims=True)
            value = jnp.sum(value, axis=1, keepdims=True)
            row = jnp.where(lane1 == c * 8 + i, value, row)
        return row

    mine[0] = lax.fori_loop(0, channels, moments, jnp.zeros((1, LANES), jnp.float32))

    def sum_copy(other, slot):
        return pltpu.make_async_remote_copy(
            src_ref=mine.at[0],
            dst_ref=sums.at[slot],
            send_sem=sum_send_sem.at[other],
            recv_sem=sum_recv_sem.at[slot],
            device_id={"tm": other},
        )

    def tell(step, carry):
        other = partner(me, step, count)

        @pl.when(other != me)
        def _():
            sum_copy(other, me).start()

        return carry

    lax.fori_loop(0, count, tell, 0)
    sums[me] = mine[0]

    def hear(step, carry):
        other = lax.rem(me + step, count)
        sum_copy(other, other).wait_recv()
        return carry

    lax.fori_loop(1, count, hear, 0)
    total = sums[0]
    for other in range(1, count):
        total = total + sums[other]
    moment = [total if i == 0 else pltpu.roll(total, LANES - i, 1) for i in range(6)]
    weights = coefficients(moment)
    spread = [
        [
            jnp.sum(jnp.where(lane1 == c * 8, w, 0.0), axis=1, keepdims=True).reshape(1, 1, 1)
            for w in weights
        ]
        for c in range(channels)
    ]

    def copy2(slot, dest, where):
        return pltpu.make_async_remote_copy(
            src_ref=send2.at[slot],
            dst_ref=recv2.at[where],
            send_sem=send2_sem.at[slot],
            recv_sem=recv2_sem.at[where],
            device_id={"tm": dest},
        )

    def give(step, carry):
        slot = lax.rem(lax.rem(me, bands) + bands // 2 + step, bands)
        dest = core * bands + slot
        start = shift + slot * band + 1
        for c in range(channels):
            result = spread[c][0] * power0[c, pl.ds(start, band)]
            result = result + spread[c][1] * power1[c, pl.ds(start, band)]
            result = result + spread[c][2] * power2[c, pl.ds(start, band)]
            send2[slot, c] = result.astype(jnp.bfloat16)

        @pl.when(dest != me)
        def _():
            copy2(slot, dest, chip).start()

        @pl.when(dest == me)
        def _():
            pltpu.make_async_copy(send2.at[slot], recv2.at[chip], local_sem.at[1]).start()

        return carry

    lax.fori_loop(0, bands, give, 0)

    def drain(step, carry):
        other = lax.rem(me + step, count)
        copy1(other).wait_send()
        sum_copy(other, me).wait_send()
        return carry

    lax.fori_loop(1, count, drain, 0)

    giver_core = me // bands

    def take(k, carry):
        giver = 2 * k + giver_core

        @pl.when(giver != me)
        def _():
            copy2(0, giver, k).wait_recv()

        @pl.when(giver == me)
        def _():
            pltpu.make_async_copy(send2.at[0], recv2.at[k], local_sem.at[1]).wait()

        return carry

    lax.fori_loop(0, chips, take, 0)
    def finish(slot, carry):
        dest = core * bands + slot

        @pl.when(dest != me)
        def _():
            copy2(slot, dest, chip).wait_send()

        return carry

    lax.fori_loop(0, bands, finish, 0)


def assemble(own, recv2, out_ref):
    frames, channels, band, cols = out_ref.shape
    for start, size in blocks_of(cols, LANES):
        column = start + lax.broadcasted_iota(jnp.int32, (frames, LANES), 1)
        for c in range(channels):
            for r in range(band):
                tile = jnp.zeros((frames, LANES), jnp.float32)
                for k in range(start // own, (start + size - 1) // own + 1):
                    piece = recv2[k, c, r].astype(jnp.float32)
                    turn = (own * k - HALO - start) % LANES
                    piece = pltpu.roll(piece, turn, 1) if turn else piece
                    tile = jnp.where(column >= own * k, piece, tile)
                out_ref[:, c, r, start:start + size] = tile[:, :size]


def shards(count, video, w_in, b_in, w_out, b_out, screen):
    _, channels, rows, cols = video.shape
    chips, band = count // 2, rows // count
    window = rows // 2 + ITERS
    chunk = -(-channels * window // 16) * 16
    f32, bf16 = jnp.float32, jnp.bfloat16
    field = pltpu.VMEM((channels, window + 2, count, LANES), f32)
    dma = pltpu.SemaphoreType.DMA
    out = pl.pallas_call(
        functools.partial(kernel, count),
        out_shape=jax.ShapeDtypeStruct((chips, channels, band, count, LANES), bf16),
        in_specs=[pl.BlockSpec(memory_space=pl.ANY)] * 6,
        out_specs=pl.BlockSpec(memory_space=pl.ANY),
        scratch_shapes=[
            pltpu.VMEM(video.shape, video.dtype),
            pltpu.SMEM(w_in.shape[::-1], f32),
            pltpu.SMEM(b_in.shape, f32),
            pltpu.SMEM(w_out.shape, f32),
            pltpu.SMEM(b_out.shape, f32),
            pltpu.SMEM(screen.shape, f32),
            dma((6,)),
            pltpu.VMEM((channels, rows, (-(-cols // LANES) + 2) * LANES), f32),
            pltpu.VMEM((chips, channels, rows, LANES), f32),
            pltpu.VMEM((2, chunk, LANES), f32),
            pltpu.VMEM((count, chunk, LANES), bf16),
            pltpu.VMEM((count, chunk, LANES), bf16),
            pltpu.VMEM((count * chunk, LANES), f32),
            field, field, field,
            pltpu.VMEM((1, 1, LANES), f32),
            pltpu.VMEM((count, 1, LANES), f32),
            pltpu.VMEM((count // 2, channels, band, count, LANES), bf16),
            dma((count,)), dma((count,)), dma((count,)), dma((count,)),
            dma((count // 2,)), dma((chips,)), dma((2,)),
        ],
        compiler_params=pltpu.CompilerParams(collective_id=0, has_side_effects=True),
    )(video, w_in.T, b_in, w_out, b_out, screen)
    return pl.pallas_call(
        functools.partial(assemble, cols // chips),
        out_shape=jax.ShapeDtypeStruct((count, channels, band, cols), f32),
        in_specs=[pl.BlockSpec(memory_space=pltpu.VMEM)],
        out_specs=pl.BlockSpec(memory_space=pltpu.VMEM),
    )(out)


def solution(mesh):
    in_specs = (P(("video", "tm"), None, None, None), P(), P(), P(), P(), P())
    out_specs = P("video", None, "tm", None)
    body = functools.partial(shards, mesh.shape["tm"])
    return jax.shard_map(body, mesh=mesh, in_specs=in_specs, out_specs=out_specs, check_vma=False)
```

profile of v0, /device:TPU:0, one launch (start us, length us, event | category | flops | bytes accessed | tf_op | source)
XLA Modules:
  0.0 28.2 jit_solution(8256208139433856811)
XLA Ops:
  0.0 26.2 %shard_map.64.recv2 = bf16[8,3,2,16,128]{4,3,2,1,0:T(8,128)(2,1)} custom-call(bf16[1,3,32,960]{3,2,1,0:T(8,128)(2,1)} %video_hbm.1, f32[3,32]{1,0:T(4,128)} %bitcast.1, f32[32]{0:T(128)} %b_in_hbm.1, f32[3,32]{1,0:T(4,128)} %w_out_hbm.1, f32[3]{0:T(128)} %b_out_hbm.1, f32[3]{0:T(128)} %screen_hbm.1), custom_call_target="tpu_custom_call" | custom-call | tf_op jit(solution)/shard_map/pallas_call | solution.py:392
  26.2 2.0 %shard_map.65 = f32[16,3,2,960]{3,2,1,0:T(2,128)} custom-call(bf16[8,3,2,16,128]{4,3,2,1,0:T(8,128)(2,1)} %shard_map.64.recv2), custom_call_target="tpu_custom_call" | custom-call | tf_op jit(solution)/shard_map/pallas_call | solution.py:420
where the time goes:
time: 28.3 us; the launch traced here: 28.2 us
  Pallas kernels  28.2 us (100%)
    pallas_call x1, Pallas kernels, shards(): pl.pallas_call(functools.partial(kernel, count), out_shape=jax.ShapeDtype...  26.2 us
    pallas_call x1, Pallas kernels, shards(): pl.pallas_call(functools.partial(assemble, cols // chips), out_shape=jax....  1.97 us

commit v1 on v0

--- a/solution.py
+++ b/solution.py
@@ -64,7 +64,7 @@
 ):
     me = lax.axis_index("tm")
     chips = count // 2
-    chip, core = me // 2, lax.rem(me, 2)
+    chip, core = lax.rem(me, chips), me // chips
     _, channels, rows, cols = video_ref.shape
     units = w_in_ref.shape[1]
     frames = count
@@ -166,7 +166,7 @@
 
     def launch(k):
         for side in range(2):
-            dest = 2 * k + side
+            dest = side * chips + k
 
             @pl.when(dest != me)
             def _():
@@ -176,7 +176,7 @@
         k = lax.rem(chip + chips // 2 + step, chips)
         grade(k)
         for side in range(2):
-            send1[2 * k + side] = packed[side].astype(jnp.bfloat16)
+            send1[side * chips + k] = packed[side].astype(jnp.bfloat16)
 
         @pl.when(step == held)
         def _():
@@ -338,10 +338,8 @@
 
     lax.fori_loop(1, count, drain, 0)
 
-    giver_core = me // bands
-
     def take(k, carry):
-        giver = 2 * k + giver_core
+        giver = core * chips + k
 
         @pl.when(giver != me)
         def _():

time: 28.3 us -> 26.4 us (0.933)
  Pallas kernels: 28.2 us -> 26.3 us
    pallas_call x1, Pallas kernels: 26.2 us -> 24.3 us  [shards(): pl.pallas_call(functools.partial(kernel, count), out_shape=jax.ShapeDtype...]
where the time goes in v1:
time: 26.4 us; the launch traced here: 26.3 us
  Pallas kernels  26.3 us (100%)
    pallas_call x1, Pallas kernels, shards(): pl.pallas_call(functools.partial(kernel, count), out_shape=jax.ShapeDtype...  24.3 us
    pallas_call x1, Pallas kernels, shards(): pl.pallas_call(functools.partial(assemble, cols // chips), out_shape=jax....  1.97 us

profile of v1, /device:TPU:0, one launch (start us, length us, event | category | flops | bytes accessed | tf_op | source)
XLA Modules:
  0.0 26.3 jit_solution(13772432291511281030)
XLA Ops:
  0.0 24.3 %shard_map.64.recv2 = bf16[8,3,2,16,128]{4,3,2,1,0:T(8,128)(2,1)} custom-call(bf16[1,3,32,960]{3,2,1,0:T(8,128)(2,1)} %video_hbm.1, f32[3,32]{1,0:T(4,128)} %bitcast.1, f32[32]{0:T(128)} %b_in_hbm.1, f32[3,32]{1,0:T(4,128)} %w_out_hbm.1, f32[3]{0:T(128)} %b_out_hbm.1, f32[3]{0:T(128)} %screen_hbm.1), custom_call_target="tpu_custom_call" | custom-call | tf_op jit(solution)/shard_map/pallas_call | solution.py:390
  24.3 2.0 %shard_map.65 = f32[16,3,2,960]{3,2,1,0:T(2,128)} custom-call(bf16[8,3,2,16,128]{4,3,2,1,0:T(8,128)(2,1)} %shard_map.64.recv2), custom_call_target="tpu_custom_call" | custom-call | tf_op jit(solution)/shard_map/pallas_call | solution.py:418

commit v2 on v1

--- a/solution.py
+++ b/solution.py
@@ -81,6 +81,8 @@
         pl.semaphore_signal(barrier, inc=1, device_id={"tm": lax.rem(me + step, count)})
         return carry
 
+    lax.fori_loop(1, count, greet, 0)
+
     loads = [
         pltpu.make_async_copy(source, dest, load_sem.at[i])
         for i, (source, dest) in enumerate(
@@ -96,7 +98,6 @@
     ]
     for load in loads:
         load.start()
-    lax.fori_loop(1, count, greet, 0)
     for load in loads:
         load.wait()
 
@@ -309,7 +310,7 @@
         )
 
     def give(step, carry):
-        slot = lax.rem(lax.rem(me, bands) + bands // 2 + step, bands)
+        slot = step
         dest = core * bands + slot
         start = shift + slot * band + 1
         for c in range(channels):
@@ -413,13 +414,14 @@
             dma((count,)), dma((count,)), dma((count,)), dma((count,)),
             dma((count // 2,)), dma((chips,)), dma((2,)),
         ],
-        compiler_params=pltpu.CompilerParams(collective_id=0, has_side_effects=True),
-    )(video, w_in.T, b_in, w_out, b_out, screen)
+        compiler_params=pltpu.CompilerParams(collective_id=0, has_side_effects=True, vmem_limit_bytes=60 << 20),
+    )(*[pltpu.with_memory_space_constraint(a, pltpu.HBM) for a in (video, w_in.T, b_in, w_out, b_out, screen)])
     return pl.pallas_call(
         functools.partial(assemble, cols // chips),
         out_shape=jax.ShapeDtypeStruct((count, channels, band, cols), f32),
         in_specs=[pl.BlockSpec(memory_space=pltpu.VMEM)],
         out_specs=pl.BlockSpec(memory_space=pltpu.VMEM),
+        compiler_params=pltpu.CompilerParams(vmem_limit_bytes=8 << 20),
     )(out)
 
 

time: 26.4 us -> 26.3 us (level)
  Pallas kernels: 26.3 us -> 25.2 us
  local copies, waits for them, and re-layouts: 0 us -> 0.92 us
    pallas_call x1, Pallas kernels: 1.97 us -> 1.05 us  [shards(): pl.pallas_call(functools.partial(assemble, cols // chips), out_shape=jax....]
    unnamed x0 -> x2, local copies, waits for them, and re-layouts: none -> 0.92 us
where the time goes in v2:
time: 26.3 us; the launch traced here: 26.1 us
  Pallas kernels  25.2 us (96%)
  local copies, waits for them, and re-layouts  0.92 us (3%)
    pallas_call x1, Pallas kernels, shards(): pl.pallas_call(functools.partial(kernel, count), out_shape=jax.ShapeDtype...  24.1 us
    pallas_call x1, Pallas kernels, shards(): pl.pallas_call(functools.partial(assemble, cols // chips), out_shape=jax....  1.05 us
    unnamed x2, local copies, waits for them, and re-layouts  0.92 us

profile of v2, /device:TPU:0, one launch (start us, length us, event | category | flops | bytes accessed | tf_op | source)
XLA Modules:
  0.0 26.1 jit_solution(16563954433529269342)
XLA Ops:
  0.0 24.1 %shard_map.64.recv2 = bf16[8,3,2,16,128]{4,3,2,1,0:T(8,128)(2,1)} custom-call(bf16[1,3,32,960]{3,2,1,0:T(8,128)(2,1)} %video_hbm.1, f32[3,32]{1,0:T(4,128)} %bitcast.1, f32[32]{0:T(128)} %b_in_hbm.1, f32[3,32]{1,0:T(4,128)} %w_out_hbm.1, f32[3]{0:T(128)} %b_out_hbm.1, f32[3]{0:T(128)} %screen_hbm.1), custom_call_target="tpu_custom_call" | custom-call | tf_op jit(solution)/shard_map/pallas_call | solution.py:391
  24.1 0.0 copy-start
  24.1 0.9 %copy-done = bf16[8,3,2,16,128]{4,3,2,1,0:T(8,128)(2,1)S(1)} copy-done((bf16[8,3,2,16,128]{4,3,2,1,0:T(8,128)(2,1)S(1)}, bf16[8,3,2,16,128]{4,3,2,1,0:T(8,128)(2,1)}, u32[]{:S(2)}) %copy-start) | copy-done | bytes 196632
  25.1 1.1 %shard_map.65 = f32[16,3,2,960]{3,2,1,0:T(2,128)} custom-call(bf16[8,3,2,16,128]{4,3,2,1,0:T(8,128)(2,1)S(1)} %copy-done), custom_call_target="tpu_custom_call" | custom-call | tf_op jit(solution)/shard_map/pallas_call | solution.py:419
Async XLA Ops:
  24.1 0.9 %copy-start = (bf16[8,3,2,16,128]{4,3,2,1,0:T(8,128)(2,1)S(1)}, bf16[8,3,2,16,128]{4,3,2,1,0:T(8,128)(2,1)}, u32[]{:S(2)}) copy-start(bf16[8,3,2,16,128]{4,3,2,1,0:T(8,128)(2,1)} %shard_map.64.recv2) | copy-start | bytes 589828

commit v3 on v2

--- a/solution.py
+++ b/solution.py
@@ -58,7 +58,7 @@
     video_hbm, w_in_hbm, b_in_hbm, w_out_hbm, b_out_hbm, screen_hbm,
     recv2,
     video_ref, w_in_ref, b_in_ref, w_out_ref, b_out_ref, screen_ref, load_sem,
-    wide, pieces, packed, send1, recv1, flat, power0, power1, power2,
+    wide, packed, send1, recv1, power0, power1, power2, power3, field1, field2, masks,
     mine, sums, send2,
     send1_sem, recv1_sem, sum_send_sem, sum_recv_sem, send2_sem, recv2_sem, local_sem,
 ):
@@ -71,6 +71,7 @@
     own = cols // chips
     half = rows // 2
     window = half + ITERS
+    pitch = window + 2
     chunk = send1.shape[1]
     band = rows // count
     bands = count // 2
@@ -117,7 +118,7 @@
                 first = pltpu.roll(first, LANES - offset, 1)
                 second = pltpu.roll(second, LANES - offset, 1)
                 first = jnp.where(lane2 < LANES - offset, first, second)
-            pieces[k, c] = first
+            field1[(k * channels + c) * rows:(k * channels + c + 1) * rows, :] = first
     packed[...] = jnp.zeros_like(packed)
 
     def grade(k):
@@ -125,7 +126,10 @@
         inside = jnp.logical_and(column >= 0, column < cols)
         parts = [[] for _ in range(channels)]
         for start, size in blocks_of(rows, 32):
-            pixels = [pieces[k, c, start:start + size, :] for c in range(channels)]
+            pixels = [
+                field1[pl.ds(pl.multiple_of((k * channels + c) * rows + start, 8), size), :]
+                for c in range(channels)
+            ]
             total = [pixels[c] + b_out_ref[c] for c in range(channels)]
             for j in range(units):
                 h = pixels[0] * (0.5 * w_in_ref[0, j]) + 0.5 * b_in_ref[j]
@@ -142,8 +146,9 @@
             beside = shifted(graded, 0, 1) + shifted(graded, 0, -1)
             beside = beside + pltpu.roll(graded, 1, 1) + pltpu.roll(graded, LANES - 1, 1)
             target = jnp.where(inside, (screen_ref[c] + 4.0) * graded - beside, 0.0)
-            packed[0, c * window:(c + 1) * window, :] = target[:window]
-            packed[1, c * window:(c + 1) * window, :] = target[rows - window:]
+            first = c * pitch + 1
+            packed[0, first:first + window, :] = target[:window]
+            packed[1, first:first + window, :] = target[rows - window:]
 
     def copy1(dest):
         return pltpu.make_async_remote_copy(
@@ -191,74 +196,105 @@
 
         return carry
 
-    lax.fori_loop(0, chips, make, 0)
-    recv1[me] = send1[me]
-
-    def land(step, carry):
-        source = lax.rem(me + step, count)
-
-        @pl.when(step > 0)
-        def _():
-            arrival1(source).wait_recv()
-
-        flat[pl.ds(pl.multiple_of(source * chunk, chunk), chunk), :] = recv1[source].astype(jnp.float32)
-        return carry
-
-    lax.fori_loop(0, count, land, 0)
-
-    lane = lax.broadcasted_iota(jnp.int32, (1, frames, LANES), 2)
+    line = lax.broadcasted_iota(jnp.int32, (chunk, LANES), 0)
+    lane = lax.broadcasted_iota(jnp.int32, (chunk, LANES), 1)
     column = lane + (own * chip - HALO)
     inside = jnp.logical_and(column >= 0, column < cols)
     owned = jnp.logical_and(lane >= HALO, lane < HALO + own)
-    frame = lax.broadcasted_iota(jnp.int32, (1, frames, LANES), 1)
-
-    for power in (power0, power1, power2):
+    shift = core * ITERS
+    weight = jnp.zeros((chunk, LANES), jnp.float32)
+    kept = jnp.zeros((chunk, LANES), jnp.float32)
+    for c in range(channels):
+        rows_of = jnp.logical_and(line >= c * pitch + 1, line < c * pitch + 1 + window)
+        kept = jnp.where(jnp.logical_and(rows_of, inside), 1.0, kept)
+        weight = jnp.where(rows_of, 6.0 + screen_ref[c], weight)
+        start = c * pitch + 1 + shift
+        mine_of = jnp.logical_and(line >= start, line < start + half)
+        masks[2 + c] = jnp.where(jnp.logical_and(mine_of, owned), 1.0, 0.0)
+    masks[0] = weight
+    masks[1] = kept
+
+    lax.fori_loop(0, chips, make, 0)
+    recv1[me] = send1[me]
+
+    def within(field):
+        total = pltpu.roll(field, 1, 0) + pltpu.roll(field, chunk - 1, 0)
+        total = total + pltpu.roll(field, 1, 1) + pltpu.roll(field, LANES - 1, 1)
+        return (masks[0] * field - total) * masks[1]
+
+    def land(step, carry):
+        k = lax.rem(chip + chips // 2 + chips - step, chips)
+        near, far = core * chips + k, (1 - core) * chips + k
+
+        @pl.when(near != me)
+        def _():
+            arrival1(near).wait_recv()
+
+        arrival1(far).wait_recv()
+        sources = (near, far)
+        spots = [pl.ds(pl.multiple_of(source * chunk, chunk), chunk) for source in sources]
+        fields = [recv1[source].astype(jnp.float32) for source in sources]
+        for spot, field in zip(spots, fields):
+            power0[spot, :] = field
+        for power in (power1, power2, power3):
+            fields = [within(field) for field in fields]
+            for spot, field in zip(spots, fields):
+                power[spot, :] = field
+        return carry
+
+    lax.fori_loop(0, chips, land, 0)
+
+    def beside(terms, f):
+        if f == 0:
+            return terms[1]
+        if f == frames - 1:
+            return terms[f - 1]
+        return terms[f - 1] + terms[f + 1]
+
+    def moments(block, totals):
+        def at(ref, f):
+            return ref[pl.ds(pl.multiple_of(f * chunk + block * 8, 8), 8), :]
+
+        p0, p1, p2, v1, g, e, v2, h = ({} for _ in range(8))
+        acc = [jnp.zeros((8, LANES), jnp.float32) for _ in range(6)]
+        p0[0], p1[0] = at(power0, 0), at(power1, 0)
+        for t in range(frames + 2):
+            if t < frames:
+                if t + 1 < frames:
+                    p0[t + 1], p1[t + 1] = at(power0, t + 1), at(power1, t + 1)
+                p2[t] = at(power2, t)
+                v1[t] = p1[t] - beside(p0, t)
+                g[t] = p2[t] - beside(p1, t)
+                e[t] = p2[t] + g[t]
+                field1[pl.ds(pl.multiple_of(t * chunk + block * 8, 8), 8), :] = v1[t]
+            u = t - 1
+            if 0 <= u < frames:
+                v2[u] = g[u] - beside(v1, u)
+                h[u] = at(power3, u) - beside(e, u)
+                field2[pl.ds(pl.multiple_of(u * chunk + block * 8, 8), 8), :] = v2[u]
+            w = t - 2
+            if 0 <= w < frames:
+                v3 = h[w] - beside(v2, w)
+                pairs = ((p0[w], p0[w]), (p0[w], v1[w]), (v1[w], v1[w]), (v1[w], v2[w]), (v2[w], v2[w]), (v2[w], v3))
+                for i, (left, right) in enumerate(pairs):
+                    acc[i] = acc[i] + left * right
+        result = []
         for c in range(channels):
-            power[c, 0] = jnp.zeros((frames, LANES), jnp.float32)
-            power[c, window + 1] = jnp.zeros((frames, LANES), jnp.float32)
+            mask = masks[2 + c, pl.ds(pl.multiple_of(block * 8, 8), 8), :]
+            for i in range(6):
+                result.append(totals[c * 6 + i] + mask * acc[i])
+        return tuple(result)
+
+    lane1 = lax.broadcasted_iota(jnp.int32, (1, LANES), 1)
+    zero = jnp.zeros((8, LANES), jnp.float32)
+    totals = lax.fori_loop(0, chunk // 8, moments, (zero,) * (6 * channels))
+    row = jnp.zeros((1, LANES), jnp.float32)
     for c in range(channels):
-        for r in range(window):
-            power0[c, r + 1] = flat[pl.ds(c * window + r, frames, chunk), :]
-
-    def operate(ref, c, start, size):
-        whole = ref[c, pl.ds(start, size + 2)]
-        centre = whole[1:size + 1]
-        total = whole[:size] + whole[2:]
-        total = total + pltpu.roll(centre, 1, 2) + pltpu.roll(centre, LANES - 1, 2)
-        before = jnp.where(frame == 0, 0.0, pltpu.roll(centre, 1, 1))
-        after = jnp.where(frame == frames - 1, 0.0, pltpu.roll(centre, frames - 1, 1))
-        total = total + before + after
-        return centre, (6.0 + screen_ref[c]) * centre - total
-
-    shift = core * ITERS
-    for ref, result in ((power0, power1), (power1, power2)):
-        def apply(c, carry, ref=ref, result=result):
-            for start, size in blocks_of(window, 4):
-                _, image = operate(ref, c, start, size)
-                result[c, start + 1:start + 1 + size] = jnp.where(inside, image, 0.0)
-            return carry
-
-        lax.fori_loop(0, channels, apply, 0)
-
-    lane1 = lax.broadcasted_iota(jnp.int32, (1, LANES), 1)
-
-    def moments(c, row):
-        acc = [jnp.zeros((frames, LANES), jnp.float32) for _ in range(6)]
-        for start, size in blocks_of(half, 4):
-            v0 = power0[c, pl.ds(shift + start + 1, size)]
-            v1 = power1[c, pl.ds(shift + start + 1, size)]
-            v2, v3 = operate(power2, c, shift + start, size)
-            for i, (left, right) in enumerate(
-                ((v0, v0), (v0, v1), (v1, v1), (v1, v2), (v2, v2), (v2, v3))
-            ):
-                acc[i] = acc[i] + jnp.sum(left * right, axis=0)
         for i in range(6):
-            value = jnp.sum(jnp.where(owned[0], acc[i], 0.0), axis=0, keepdims=True)
+            value = jnp.sum(totals[c * 6 + i], axis=0, keepdims=True)
             value = jnp.sum(value, axis=1, keepdims=True)
             row = jnp.where(lane1 == c * 8 + i, value, row)
-        return row
-
-    mine[0] = lax.fori_loop(0, channels, moments, jnp.zeros((1, LANES), jnp.float32))
+    mine[0] = row
 
     def sum_copy(other, slot):
         return pltpu.make_async_remote_copy(
@@ -281,6 +317,20 @@
     lax.fori_loop(0, count, tell, 0)
     sums[me] = mine[0]
 
+    def turn(f, carry):
+        here = pl.ds(pl.multiple_of(f * chunk, chunk), chunk)
+        for field, turned in ((power0, power1), (field1, power2), (field2, power3)):
+            turned[pl.ds(f, chunk, frames), :] = field[here, :]
+        return carry
+
+    lax.fori_loop(0, frames, turn, 0)
+
+    def sent(step, carry):
+        copy1(lax.rem(me + step, count)).wait_send()
+        return carry
+
+    lax.fori_loop(1, count, sent, 0)
+
     def hear(step, carry):
         other = lax.rem(me + step, count)
         sum_copy(other, other).wait_recv()
@@ -293,10 +343,7 @@
     moment = [total if i == 0 else pltpu.roll(total, LANES - i, 1) for i in range(6)]
     weights = coefficients(moment)
     spread = [
-        [
-            jnp.sum(jnp.where(lane1 == c * 8, w, 0.0), axis=1, keepdims=True).reshape(1, 1, 1)
-            for w in weights
-        ]
+        [jnp.sum(jnp.where(lane1 == c * 8, w, 0.0), axis=1, keepdims=True) for w in weights]
         for c in range(channels)
     ]
 
@@ -312,12 +359,14 @@
     def give(step, carry):
         slot = step
         dest = core * bands + slot
-        start = shift + slot * band + 1
         for c in range(channels):
-            result = spread[c][0] * power0[c, pl.ds(start, band)]
-            result = result + spread[c][1] * power1[c, pl.ds(start, band)]
-            result = result + spread[c][2] * power2[c, pl.ds(start, band)]
-            send2[slot, c] = result.astype(jnp.bfloat16)
+            for r in range(band):
+                first = (c * pitch + 1 + shift + slot * band + r) * frames
+                here = pl.ds(pl.multiple_of(first, frames), frames)
+                result = spread[c][0] * power1[here, :]
+                result = result + spread[c][1] * power2[here, :]
+                result = result + spread[c][2] * power3[here, :]
+                send2[slot, c, r] = result.astype(jnp.bfloat16)
 
         @pl.when(dest != me)
         def _():
@@ -333,7 +382,6 @@
 
     def drain(step, carry):
         other = lax.rem(me + step, count)
-        copy1(other).wait_send()
         sum_copy(other, me).wait_send()
         return carry
 
@@ -384,10 +432,13 @@
     _, channels, rows, cols = video.shape
     chips, band = count // 2, rows // count
     window = rows // 2 + ITERS
-    chunk = -(-channels * window // 16) * 16
+    chunk = -(-channels * (window + 2) // 16) * 16
     f32, bf16 = jnp.float32, jnp.bfloat16
-    field = pltpu.VMEM((channels, window + 2, count, LANES), f32)
+    field = pltpu.VMEM((count * chunk, LANES), f32)
     dma = pltpu.SemaphoreType.DMA
+    held = 4 * (6 * count * chunk + (2 + channels + count) * chunk)
+    held = LANES * (held + 8 * channels * count * count)
+    limit = min(60 << 20, max(24 << 20, held + (8 << 20)))
     out = pl.pallas_call(
         functools.partial(kernel, count),
         out_shape=jax.ShapeDtypeStruct((chips, channels, band, count, LANES), bf16),
@@ -402,19 +453,18 @@
             pltpu.SMEM(screen.shape, f32),
             dma((6,)),
             pltpu.VMEM((channels, rows, (-(-cols // LANES) + 2) * LANES), f32),
-            pltpu.VMEM((chips, channels, rows, LANES), f32),
             pltpu.VMEM((2, chunk, LANES), f32),
             pltpu.VMEM((count, chunk, LANES), bf16),
             pltpu.VMEM((count, chunk, LANES), bf16),
-            pltpu.VMEM((count * chunk, LANES), f32),
-            field, field, field,
+            field, field, field, field, field, field,
+            pltpu.VMEM((2 + channels, chunk, LANES), f32),
             pltpu.VMEM((1, 1, LANES), f32),
             pltpu.VMEM((count, 1, LANES), f32),
             pltpu.VMEM((count // 2, channels, band, count, LANES), bf16),
             dma((count,)), dma((count,)), dma((count,)), dma((count,)),
             dma((count // 2,)), dma((chips,)), dma((2,)),
         ],
-        compiler_params=pltpu.CompilerParams(collective_id=0, has_side_effects=True, vmem_limit_bytes=60 << 20),
+        compiler_params=pltpu.CompilerParams(collective_id=0, has_side_effects=True, vmem_limit_bytes=limit),
     )(*[pltpu.with_memory_space_constraint(a, pltpu.HBM) for a in (video, w_in.T, b_in, w_out, b_out, screen)])
     return pl.pallas_call(
         functools.partial(assemble, cols // chips),

time: 26.3 us -> 24.5 us (0.932)
  local copies, waits for them, and re-layouts: 0.92 us -> 0 us
  Pallas kernels: 25.2 us -> 24.3 us
    unnamed x2 -> x0, local copies, waits for them, and re-layouts: 0.92 us -> none
    pallas_call x1, Pallas kernels: 24.1 us -> 23.3 us  [shards(): pl.pallas_call(functools.partial(kernel, count), out_shape=jax.ShapeDtype...]
where the time goes in v3:
time: 24.5 us; the launch traced here: 24.3 us
  Pallas kernels  24.3 us (99%)
    pallas_call x1, Pallas kernels, shards(): pl.pallas_call(functools.partial(kernel, count), out_shape=jax.ShapeDtype...  23.3 us
    pallas_call x1, Pallas kernels, shards(): pl.pallas_call(functools.partial(assemble, cols // chips), out_shape=jax....  1.05 us

profile of v3, /device:TPU:0, one launch (start us, length us, event | category | flops | bytes accessed | tf_op | source)
XLA Modules:
  0.0 24.3 jit_solution(10002506298280919356)
XLA Ops:
  0.0 23.3 %shard_map.64.recv2 = bf16[8,3,2,16,128]{4,3,2,1,0:T(8,128)(2,1)S(1)} custom-call(bf16[1,3,32,960]{3,2,1,0:T(8,128)(2,1)} %video_hbm.1, f32[3,32]{1,0:T(4,128)} %bitcast.1, f32[32]{0:T(128)} %b_in_hbm.1, f32[3,32]{1,0:T(4,128)} %w_out_hbm.1, f32[3]{0:T(128)} %b_out_hbm.1, f32[3]{0:T(128)} %screen_hbm.1), custom_call_target="tpu_custom_call" | custom-call | tf_op jit(solution)/shard_map/pallas_call | solution.py:442
  23.3 1.1 %shard_map.65 = f32[16,3,2,960]{3,2,1,0:T(2,128)} custom-call(bf16[8,3,2,16,128]{4,3,2,1,0:T(8,128)(2,1)S(1)} %shard_map.64.recv2), custom_call_target="tpu_custom_call" | custom-call | tf_op jit(solution)/shard_map/pallas_call | solution.py:469
